TPU v7x, 32 devices: a whole 2x2x4 slice. The times are simulated.
32 devices in a mesh: group: 4 (over y, x), member: 8 (over z, core).
Axes of the slice: x: 2, y: 2, z: 4, core: 2. Of those that a mesh axis runs over, the one named last changes fastest.
Arguments:
- activations: bfloat16 [4, 1024, 2048], P('group', 'member'), may hold values from -6 to 6
- lengths: int32 [4, 8], P('group'), may hold values from 1 to 128, 576 in all within a row
- assignment: int32 [4, 8], P('group'), may hold values from 0 to 7, each once within a row
- owners: int32 [4], replicated, may hold values from 0 to 3
- prefix_cache: bfloat16 [4, 8192, 256], P('group', 'member'), may hold values from -244 to 244
- first_gain: float32 [2048], replicated, may hold values from 0.1 to 1.9
- first_bias: float32 [2048], replicated, may hold values from -3 to 3
- query_weight: bfloat16 [2048, 2048], replicated, may hold values from -0.125 to 0.125
- keyval_weight: bfloat16 [2048, 256], replicated, may hold values from -0.4375 to 0.4375
- output_weight: bfloat16 [2048, 2048], replicated, may hold values from -0.125 to 0.125
- second_gain: float32 [2048], replicated, may hold values from 0.1 to 1.9
- second_bias: float32 [2048], replicated, may hold values from -3 to 3
- expand_weight: bfloat16 [2048, 8192], P(None, 'member'), may hold values from -0.125 to 0.125
- contract_weight: bfloat16 [8192, 2048], P('member'), may hold values from -0.0625 to 0.0625
Outputs:
- layer_output: bfloat16 [4, 1024, 2048], P('group', 'member')
Inputs may be any that keep to these rules, and one draw needn't show every extreme that they name: Each row of lengths sums to 576 and its longest entry is 128. Each row of assignment names every request of its group once. `owners`: several groups may attend the same cache slot.
All inputs are finite; a program needn't handle non-finite values.
Results may differ from a plain program's by a relative error of at most 0.011.
The roundings to bfloat16 on the way count: a program that leaves them out, or rounds other values in their place, can miss the bound.
Values may be sent and summed in bfloat16 or wider, within the bound.
No kernel may reach another device: no remote copies, remote signals or barrier semaphores. Data moves between devices by JAX's collectives and lax.ppermute only.
A program may use at most 128 MiB of HBM per device.

v0:
```python
import math
import jax
import jax.numpy as jnp
from jax import lax
from jax.sharding import PartitionSpec as P

EPSILON = 1e-05
NEGATIVE = -1e30


def layer_norm(values, gain, bias):
    average = jnp.mean(values, axis=-1, keepdims=True)
    centered = values - average
    spread = jnp.mean(centered * centered, axis=-1, keepdims=True)
    return centered * lax.rsqrt(spread + EPSILON) * gain + bias


def pick_value(table, wanted):
    slots_at = lax.broadcasted_iota(jnp.int32, table.shape, 0)
    return jnp.sum(jnp.where(slots_at == wanted, table, 0))


def own_scores(query_block, own_keys, scaling):
    scores = (
        jnp.einsum("thd,sd->ths", query_block, own_keys, preferred_element_type=jnp.float32)
        * scaling
    )
    block_rows = query_block.shape[0]
    key_rows = own_keys.shape[0]
    row_at = lax.broadcasted_iota(jnp.int32, (block_rows, 1, key_rows), 0)
    column_at = lax.broadcasted_iota(jnp.int32, (block_rows, 1, key_rows), 2)
    return jnp.where(column_at <= row_at, scores, NEGATIVE)


def folded_attention(queries, keys_values, selected):
    row_count, head_count, head_size = queries.shape
    scaling = 1.0 / math.sqrt(head_size)
    own_keys = keys_values[:, :head_size]
    own_values = keys_values[:, head_size:]
    suffix_scores = own_scores(queries, own_keys, scaling)
    highest = jnp.max(suffix_scores, axis=-1)
    suffix_exp = jnp.exp(suffix_scores - highest[..., None])
    denominator = jnp.sum(suffix_exp, axis=-1)
    weighted = jnp.einsum(
        "ths,sd->thd",
        suffix_exp.astype(jnp.bfloat16),
        own_values,
        preferred_element_type=jnp.float32,
    )
    running = (weighted, highest, denominator)
    portion = lax.all_gather(selected, "member", axis=0, tiled=True)
    extent = portion.shape[0]
    stride = math.gcd(extent, 1024)

    def advance(state_now, block_index):
        weighted_now, highest_now, denominator_now = state_now
        key_block = lax.dynamic_slice_in_dim(portion, block_index * stride, stride, 0)
        scores = (
            jnp.einsum(
                "thd,pd->thp", queries, key_block[:, :head_size], preferred_element_type=jnp.float32
            )
            * scaling
        )
        highest_next = jnp.maximum(highest_now, jnp.max(scores, axis=-1))
        rescale = jnp.exp(highest_now - highest_next)
        exponent = jnp.exp(scores - highest_next[..., None])
        denominator_next = denominator_now * rescale + jnp.sum(exponent, axis=-1)
        weighted_next = weighted_now * rescale[..., None] + jnp.einsum(
            "thp,pd->thd",
            exponent.astype(jnp.bfloat16),
            key_block[:, head_size:],
            preferred_element_type=jnp.float32,
        )
        return ((weighted_next, highest_next, denominator_next), None)

    running, _ = lax.scan(advance, running, jnp.arange(extent // stride, dtype=jnp.int32))
    weighted, highest, denominator = running
    return (
        (weighted / denominator[..., None])
        .astype(jnp.bfloat16)
        .reshape(row_count, head_count * head_size)
    )


def shards(
    activations,
    lengths,
    assignment,
    owners,
    prefix_cache,
    first_gain,
    first_bias,
    query_weight,
    keyval_weight,
    output_weight,
    second_gain,
    second_bias,
    expand_weight,
    contract_weight,
):
    group_index = lax.axis_index("group")
    member_index = lax.axis_index("member")
    request = pick_value(assignment[0], member_index)
    length_here = pick_value(lengths[0], request)
    owner_here = pick_value(owners, group_index)
    tokens = activations[0]
    row_count = tokens.shape[0]
    head_size = prefix_cache.shape[2] // 2
    head_count = tokens.shape[1] // head_size
    every_block = lax.all_gather(prefix_cache, "group", axis=0, tiled=True)
    selected = lax.dynamic_index_in_dim(every_block, owner_here, 0, keepdims=False)
    tokens_wide = tokens.astype(jnp.float32)
    normed = layer_norm(tokens_wide, first_gain, first_bias).astype(jnp.bfloat16)
    queries = jnp.dot(normed, query_weight, preferred_element_type=jnp.float32).astype(jnp.bfloat16)
    queries = queries.reshape(row_count, head_count, head_size)
    keys_values = jnp.dot(normed, keyval_weight, preferred_element_type=jnp.float32).astype(
        jnp.bfloat16
    )
    attended = folded_attention(queries, keys_values, selected)
    residual = tokens_wide + jnp.dot(attended, output_weight, preferred_element_type=jnp.float32)
    second = layer_norm(residual, second_gain, second_bias).astype(jnp.bfloat16)
    hidden = jax.nn.gelu(
        jnp.dot(
            lax.all_gather(second, "member", axis=0, tiled=True),
            expand_weight,
            preferred_element_type=jnp.float32,
        ),
        approximate=True,
    ).astype(jnp.bfloat16)
    summed = lax.psum_scatter(
        jnp.dot(hidden, contract_weight, preferred_element_type=jnp.float32).astype(jnp.bfloat16),
        "member",
        scatter_dimension=0,
        tiled=True,
    ).astype(jnp.float32)
    is_live = lax.broadcasted_iota(jnp.int32, (row_count, 1), 0) < length_here
    return jnp.where(is_live, residual + summed, 0.0).astype(jnp.bfloat16)[None]


def solution(mesh):
    return jax.shard_map(
        shards,
        mesh=mesh,
        in_specs=(
            P("group", "member", None),
            P("group", None),
            P("group", None),
            P(),
            P("group", "member", None),
            P(),
            P(),
            P(),
            P(),
            P(),
            P(),
            P(),
            P(None, "member"),
            P("member", None),
        ),
        out_specs=P("group", "member", None),
        check_vma=False,
    )
```

profile of v0, /device:TPU:0, one launch (start us, length us, event | category | flops | bytes accessed | tf_op | source)
XLA Modules:
  0.0 286.6 jit_solution(2638500522030421383)
XLA Ops:
  6.5 0.7 all-gather.5.cloned.1.call-update
  7.3 1.3 fusion.43
  10.5 36.7 %all-gather.5.cloned.1.call-done = bf16[4,1024,256]{2,1,0:T(8,128)(2,1)} async-done(((bf16[1,1024,256]{2,1,0:T(8,128)(2,1)}), bf16[4,1024,256]{2,1,0:T(8,128)(2,1)}) %all-gather.5.cloned.1.call-update) | async-done | bytes 2097168 | tf_op jit(solution)/shard_map/all_gather | solution.py:110
  47.2 1.9 constant_dynamic-slice_fusion
  49.2 1.2 convert_reduce_fusion
  50.4 1.3 fusion.31
  51.8 5.0 %fusion.30 = bf16[16,16,8,128]{3,2,1,0:T(8,128)(2,1)S(1)} fusion(bf16[2048,2048]{1,0:T(8,128)(2,1)} %param.23, bf16[1,128,2048]{2,1,0:T(8,128)(2,1)} %param.16, f32[2048]{0:T(1024)} %param.22, f32[2048]{0:T(1024)} %param.21, f32[128]{0:T(128)S(1)} %add_rsqrt_fusion.1, f32[128]{0:T(128)S(1)} %broadcast_multiply_fusion.1), kind=kOutput, calls=%fused_computation.39 | convolution fusion | flops 1075576832 | bytes 9454592 | tf_op jit(solution)/shard_map/dot_general | solution.py:114
  58.2 38.3 %all-gather.9.cloned.1.call-done = bf16[1,8192,256]{2,1,0:T(8,128)(2,1)} async-done(((bf16[1,1024,256]{2,1,0:T(8,128)(2,1)}), bf16[1,8192,256]{2,1,0:T(8,128)(2,1)}) %all-gather.9.cloned.1.call-update) | async-done | bytes 4194320 | tf_op jit(solution)/shard_map/all_gather | solution.py:51
  96.4 62.7 %while.14 = (s32[]{:T(128)}, f32[128,16,128]{2,0,1:T(8,128)S(1)}, f32[128,16]{0,1:T(8,128)S(1)}, f32[128,16]{0,1:T(8,128)S(1)}, s32[8]{0:T(128)S(1)}, /*index=5*...) while((s32[]{:T(128)}, f32[128,16,128]{2,0,1:T(8,128)S(1)}, ...), condition=%wide.region_10.11_spmd, body=%wide.region_7.10_spmd.sunk | while | flops 1091047424 | bytes 28442832 | solution.py:76
  97.7 2.2 bitcast_reduce_fusion.2
  99.9 1.4 fusion.68
  101.3 2.9 %fusion.69 = f32[128,16,128]{2,0,1:T(8,128)S(1)} fusion(f32[1024,128,16]{1,0,2:T(8,128)S(1)} %get-tuple-element.135, f32[128,16]{0,1:T(8,128)S(1)} %max.4, f32[128,16,128]{2,0,1:T(8,128)S(1)} %get-tuple-element.152, f32[128,16]{0,1:T(8,128)S(1)} %get-tuple-element.137, bf16[8192,256]{1,0:T(8,128)(2,1)} %get-tuple-element.168, s32[]{:T(128)S(6)} %select_n.46, ...), kind=kOutput, calls=%fused_computation.8.clone.1 | convolution fusion | flops 543686656 | bytes 10764296 | tf_op jit(solution)/shard_map/while/body/eval_jaxpr/thp,pd->thd/dot_general | solution.py:68
  104.3 0.6 dynamic_slice.14
  105.5 2.2 bitcast_reduce_fusion.2
  107.8 1.4 fusion.68
  109.2 2.9 %fusion.69 = f32[128,16,128]{2,0,1:T(8,128)S(1)} fusion(f32[1024,128,16]{1,0,2:T(8,128)S(1)} %get-tuple-element.135, f32[128,16]{0,1:T(8,128)S(1)} %max.4, f32[128,16,128]{2,0,1:T(8,128)S(1)} %get-tuple-element.152, f32[128,16]{0,1:T(8,128)S(1)} %get-tuple-element.137, bf16[8192,256]{1,0:T(8,128)(2,1)} %get-tuple-element.168, s32[]{:T(128)S(6)} %select_n.46, ...), kind=kOutput, calls=%fused_computation.8.clone.1 | convolution fusion | flops 543686656 | bytes 10764296 | tf_op jit(solution)/shard_map/while/body/eval_jaxpr/thp,pd->thd/dot_general | solution.py:68
  112.1 0.6 dynamic_slice.14
  113.4 2.2 bitcast_reduce_fusion.2
  115.6 1.4 fusion.68
  117.0 2.9 %fusion.69 = f32[128,16,128]{2,0,1:T(8,128)S(1)} fusion(f32[1024,128,16]{1,0,2:T(8,128)S(1)} %get-tuple-element.135, f32[128,16]{0,1:T(8,128)S(1)} %max.4, f32[128,16,128]{2,0,1:T(8,128)S(1)} %get-tuple-element.152, f32[128,16]{0,1:T(8,128)S(1)} %get-tuple-element.137, bf16[8192,256]{1,0:T(8,128)(2,1)} %get-tuple-element.168, s32[]{:T(128)S(6)} %select_n.46, ...), kind=kOutput, calls=%fused_computation.8.clone.1 | convolution fusion | flops 543686656 | bytes 10764296 | tf_op jit(solution)/shard_map/while/body/eval_jaxpr/thp,pd->thd/dot_general | solution.py:68
  120.0 0.6 dynamic_slice.14
  121.2 2.2 bitcast_reduce_fusion.2
  123.4 1.4 fusion.68
  124.8 2.9 %fusion.69 = f32[128,16,128]{2,0,1:T(8,128)S(1)} fusion(f32[1024,128,16]{1,0,2:T(8,128)S(1)} %get-tuple-element.135, f32[128,16]{0,1:T(8,128)S(1)} %max.4, f32[128,16,128]{2,0,1:T(8,128)S(1)} %get-tuple-element.152, f32[128,16]{0,1:T(8,128)S(1)} %get-tuple-element.137, bf16[8192,256]{1,0:T(8,128)(2,1)} %get-tuple-element.168, s32[]{:T(128)S(6)} %select_n.46, ...), kind=kOutput, calls=%fused_computation.8.clone.1 | convolution fusion | flops 543686656 | bytes 10764296 | tf_op jit(solution)/shard_map/while/body/eval_jaxpr/thp,pd->thd/dot_general | solution.py:68
  127.8 0.6 dynamic_slice.14
  129.0 2.2 bitcast_reduce_fusion.2
  131.3 1.4 fusion.68
  132.7 2.9 %fusion.69 = f32[128,16,128]{2,0,1:T(8,128)S(1)} fusion(f32[1024,128,16]{1,0,2:T(8,128)S(1)} %get-tuple-element.135, f32[128,16]{0,1:T(8,128)S(1)} %max.4, f32[128,16,128]{2,0,1:T(8,128)S(1)} %get-tuple-element.152, f32[128,16]{0,1:T(8,128)S(1)} %get-tuple-element.137, bf16[8192,256]{1,0:T(8,128)(2,1)} %get-tuple-element.168, s32[]{:T(128)S(6)} %select_n.46, ...), kind=kOutput, calls=%fused_computation.8.clone.1 | convolution fusion | flops 543686656 | bytes 10764296 | tf_op jit(solution)/shard_map/while/body/eval_jaxpr/thp,pd->thd/dot_general | solution.py:68
  136.9 2.2 bitcast_reduce_fusion.2
  139.1 1.4 fusion.68
  140.5 2.9 %fusion.69 = f32[128,16,128]{2,0,1:T(8,128)S(1)} fusion(f32[1024,128,16]{1,0,2:T(8,128)S(1)} %get-tuple-element.135, f32[128,16]{0,1:T(8,128)S(1)} %max.4, f32[128,16,128]{2,0,1:T(8,128)S(1)} %get-tuple-element.152, f32[128,16]{0,1:T(8,128)S(1)} %get-tuple-element.137, bf16[8192,256]{1,0:T(8,128)(2,1)} %get-tuple-element.168, s32[]{:T(128)S(6)} %select_n.46, ...), kind=kOutput, calls=%fused_computation.8.clone.1 | convolution fusion | flops 543686656 | bytes 10764296 | tf_op jit(solution)/shard_map/while/body/eval_jaxpr/thp,pd->thd/dot_general | solution.py:68
  144.7 2.2 bitcast_reduce_fusion.2
  147.0 1.4 fusion.68
  148.4 2.9 %fusion.69 = f32[128,16,128]{2,0,1:T(8,128)S(1)} fusion(f32[1024,128,16]{1,0,2:T(8,128)S(1)} %get-tuple-element.135, f32[128,16]{0,1:T(8,128)S(1)} %max.4, f32[128,16,128]{2,0,1:T(8,128)S(1)} %get-tuple-element.152, f32[128,16]{0,1:T(8,128)S(1)} %get-tuple-element.137, bf16[8192,256]{1,0:T(8,128)(2,1)} %get-tuple-element.168, s32[]{:T(128)S(6)} %select_n.46, ...), kind=kOutput, calls=%fused_computation.8.clone.1 | convolution fusion | flops 543686656 | bytes 10764296 | tf_op jit(solution)/shard_map/while/body/eval_jaxpr/thp,pd->thd/dot_general | solution.py:68
  152.6 2.2 bitcast_reduce_fusion.2
  154.8 1.4 fusion.68
  156.2 2.9 %fusion.69 = f32[128,16,128]{2,0,1:T(8,128)S(1)} fusion(f32[1024,128,16]{1,0,2:T(8,128)S(1)} %get-tuple-element.135, f32[128,16]{0,1:T(8,128)S(1)} %max.4, f32[128,16,128]{2,0,1:T(8,128)S(1)} %get-tuple-element.152, f32[128,16]{0,1:T(8,128)S(1)} %get-tuple-element.137, bf16[8192,256]{1,0:T(8,128)(2,1)} %get-tuple-element.168, s32[]{:T(128)S(6)} %select_n.46, ...), kind=kOutput, calls=%fused_computation.8.clone.1 | convolution fusion | flops 543686656 | bytes 10764296 | tf_op jit(solution)/shard_map/while/body/eval_jaxpr/thp,pd->thd/dot_general | solution.py:68
  159.2 1.3 copy.28
  160.5 1.3 divide_convert_fusion
  161.9 4.8 %fusion.51 = (f32[128]{0:T(128)S(1)}, f32[128,2048]{1,0:T(8,128)S(1)}) fusion(bf16[128,2048]{0,1:T(8,128)(2,1)S(1)} %bitcast.88, bf16[2048,2048]{1,0:T(8,128)(2,1)} %param.25, bf16[1,128,2048]{2,1,0:T(8,128)(2,1)S(1)} %copy-done.1), kind=kOutput, calls=%fused_computation.76 | convolution fusion | flops 1074528128 | bytes 10486272 | tf_op jit(solution)/shard_map/dot_general | solution.py:120
  166.9 1.0 add_convert_fusion
  168.2 45.8 %all-gather.7.cloned.1.call-done = bf16[1024,2048]{1,0:T(8,128)(2,1)} async-done(((bf16[128,2048]{1,0:T(8,128)(2,1)}), bf16[1024,2048]{1,0:T(8,128)(2,1)}) %all-gather.7.cloned.1.call-update) | async-done | bytes 4194320 | tf_op jit(solution)/shard_map/all_gather | solution.py:124
  214.0 15.1 %convolution_convert_fusion = bf16[1024,2048]{1,0:T(8,128)(2,1)} fusion(bf16[1024,2048]{1,0:T(8,128)(2,1)} %param.29, bf16[1024,2048]{1,0:T(8,128)(2,1)} %all-gather.7.cloned.1.call-done, bf16[2048,1024]{1,0:T(8,128)(2,1)} %param.28), kind=kOutput, calls=%fused_computation.25 | convolution fusion | flops 8601468928 | bytes 16777216 | tf_op jit(solution)/shard_map/dot_general | solution.py:131
  229.2 0.6 copy-done.6
  229.8 0.6 fusion.41
  230.4 1.2 fusion.42
  232.2 45.8 %reduce-scatter.2.cloned.1.call-done = bf16[128,2048]{1,0:T(8,128)(2,1)} async-done(((bf16[1024,2048]{1,0:T(8,128)(2,1)}), bf16[128,2048]{1,0:T(8,128)(2,1)}) %reduce-scatter.2.cloned.1.call-update) | async-done | bytes 524304 | tf_op jit(solution)/shard_map/reduce_scatter | solution.py:130
  278.0 2.0 fusion.39
  (63 shorter events, 5.1 us)
Async XLA Ops:
  6.5 50.4 %copy-start = (bf16[2048,256]{1,0:T(8,128)(2,1)S(1)}, bf16[2048,256]{1,0:T(8,128)(2,1)}, u32[]{:S(2)}) copy-start(bf16[2048,256]{1,0:T(8,128)(2,1)} %param.24) | copy-start | bytes 3145732
  6.5 40.7 %all-gather.5.cloned.1.call-start = ((), (), s32[]{:S(2)}) async-start(), calls=%async_computation.1 | async-start | bytes 2621440 | tf_op jit(solution)/shard_map/all_gather | solution.py:110
  7.3 89.2 %all-gather.9.cloned.1.call-start = ((), (), s32[]{:S(2)}) async-start(), calls=%async_computation.4 | async-start | bytes 4718592 | tf_op jit(solution)/shard_map/all_gather | solution.py:51
  49.1 164.9 %all-gather.7.cloned.1.call-start = ((), (), s32[]{:S(2)}) async-start(), calls=%async_computation.2 | async-start | bytes 4718592 | tf_op jit(solution)/shard_map/all_gather | solution.py:124
  51.7 5.2 %copy-start.1 = (bf16[1,128,2048]{2,1,0:T(8,128)(2,1)S(1)}, bf16[1,128,2048]{2,1,0:T(8,128)(2,1)}, u32[]{:S(2)}) copy-start(bf16[1,128,2048]{2,1,0:T(8,128)(2,1)} %param.16) | copy-start | bytes 1572868
  51.7 5.2 %copy-start.4 = (f32[2048]{0:T(1024)S(1)}, f32[2048]{0:T(1024)}, u32[]{:S(2)}) copy-start(f32[2048]{0:T(1024)} %param.22) | copy-start | bytes 24580
  51.8 5.2 %copy-start.5 = (f32[2048]{0:T(1024)S(1)}, f32[2048]{0:T(1024)}, u32[]{:S(2)}) copy-start(f32[2048]{0:T(1024)} %param.21) | copy-start | bytes 24580
  161.8 5.1 %copy-start.2 = (f32[2048]{0:T(1024)S(1)}, f32[2048]{0:T(1024)}, u32[]{:S(2)}) copy-start(f32[2048]{0:T(1024)} %param.27) | copy-start | bytes 24580
  161.9 5.1 %copy-start.3 = (f32[2048]{0:T(1024)S(1)}, f32[2048]{0:T(1024)}, u32[]{:S(2)}) copy-start(f32[2048]{0:T(1024)} %param.26) | copy-start | bytes 24580
  168.0 110.1 %reduce-scatter.2.cloned.1.call-start = ((), (), s32[]{:S(2)}) async-start(), calls=%async_computation.3 | async-start | bytes 4718592 | tf_op jit(solution)/shard_map/reduce_scatter | solution.py:130
  229.1 0.7 copy-start.6
  229.1 1.3 copy-start.7
Sparse Core Ops, SparseCore 0:
  9.2 38.0 all-gather.4
  49.3 47.1 all-gather.8
  168.1 45.8 all-gather.6
  229.3 48.7 reduce-scatter.1
where the time goes:
time: 288 us; the launch traced here: 287 us
  waiting for transfers between devices  167 us (58%)
  matrix products  67.1 us (23%)
  other arithmetic  22.2 us (8%)
  between operations  15.2 us (5%)
  local copies, waits for them, and re-layouts  8.7 us (3%)
  loops' own time  5.68 us (2%)
    reduce_scatter x1, waiting for transfers between devices, shards(): lax.psum_scatter(jnp.dot(hidden, contract_weight, preferred_element_type=...  45.8 us
    all_gather x1, waiting for transfers between devices, shards(): lax.all_gather(second, 'member', axis=0, tiled=True)  45.8 us
    all_gather x1, waiting for transfers between devices, folded_attention(): portion = lax.all_gather(selected, 'member', axis=0, tiled=True)  38.3 us
    all_gather x1, waiting for transfers between devices, shards(): every_block = lax.all_gather(prefix_cache, 'group', axis=0, tiled=True)  36.7 us
    dot_general x8, matrix products, advance(): jnp.einsum('thp,pd->thd', exponent.astype(jnp.bfloat16), key_block[:, hea...  23.5 us
    dot_general x8, matrix products, advance(): jnp.einsum('thd,pd->thp', queries, key_block[:, :head_size], preferred_el...  17.7 us
    dot_general x1, matrix products, shards(): jnp.dot(hidden, contract_weight, preferred_element_type=jnp.float32)  15.1 us
    reduce_sum x8, other arithmetic, advance(): denominator_next = denominator_now * rescale + jnp.sum(exponent, axis=-1)  11 us
  transfers between devices with their start and end apart: 4, of which 4 were waited for; matrix products, arithmetic and copies ran while one was open for 4% of the time, Pallas kernels for 0%

commit v1 on v0

--- a/solution.py
+++ b/solution.py
@@ -107,7 +107,14 @@
     row_count = tokens.shape[0]
     head_size = prefix_cache.shape[2] // 2
     head_count = tokens.shape[1] // head_size
-    every_block = lax.all_gather(prefix_cache, "group", axis=0, tiled=True)
+    ring = [prefix_cache]
+    for hop in range(3):
+        ring.append(lax.ppermute(ring[-1], "group", [(dev, (dev + 1) % 4) for dev in range(4)]))
+    every_block = jnp.roll(
+        jnp.concatenate(ring[::-1], axis=0),
+        (lax.axis_index("group") + 1) * ring[0].shape[0],
+        axis=0,
+    )
     selected = lax.dynamic_index_in_dim(every_block, owner_here, 0, keepdims=False)
     tokens_wide = tokens.astype(jnp.float32)
     normed = layer_norm(tokens_wide, first_gain, first_bias).astype(jnp.bfloat16)

time: 288 us -> 292 us (1.014)
  starting transfers between devices: 0.31 us -> 3.96 us
    all_gather x1 -> x0, waiting for transfers between devices: 36.7 us -> none  [shards(): every_block = lax.all_gather(prefix_cache, 'group', axis=0, tiled=True)]
    ppermute x0 -> x3, waiting for transfers between devices: none -> 36.2 us  [shards(): lax.ppermute(ring[-1], 'group', [(dev, (dev + 1) % 4) for dev in range(4)])]
    ppermute x0 -> x3, starting transfers between devices: none -> 3.7 us  [shards(): lax.ppermute(ring[-1], 'group', [(dev, (dev + 1) % 4) for dev in range(4)])]
    unnamed x16 -> x27, local copies, waits for them, and re-layouts: 0.66 us -> 3.8 us
  transfers between devices with their start and end apart: 4 -> 6, of which waited for: 4 -> 6; matrix products, arithmetic and copies ran while one was open for 4% -> 4% of each run, Pallas kernels for 0% -> 0%
where the time goes in v1:
time: 292 us; the launch traced here: 291 us
  waiting for transfers between devices  168 us (58%)
  matrix products  66.9 us (23%)
  other arithmetic  20.1 us (7%)
  between operations  15.3 us (5%)
  local copies, waits for them, and re-layouts  10.8 us (4%)
  loops' own time  5.68 us (2%)
  starting transfers between devices  3.96 us (1%)
    reduce_scatter x1, waiting for transfers between devices, shards(): lax.psum_scatter(jnp.dot(hidden, contract_weight, preferred_element_type=...  45.8 us
    all_gather x1, waiting for transfers between devices, shards(): lax.all_gather(second, 'member', axis=0, tiled=True)  45.8 us
    all_gather x1, waiting for transfers between devices, folded_attention(): portion = lax.all_gather(selected, 'member', axis=0, tiled=True)  40.5 us
    ppermute x3, waiting for transfers between devices, shards(): lax.ppermute(ring[-1], 'group', [(dev, (dev + 1) % 4) for dev in range(4)])  36.2 us
    dot_general x8, matrix products, advance(): jnp.einsum('thp,pd->thd', exponent.astype(jnp.bfloat16), key_block[:, hea...  23.5 us
    dot_general x8, matrix products, advance(): jnp.einsum('thd,pd->thp', queries, key_block[:, :head_size], preferred_el...  17.7 us
    dot_general x1, matrix products, shards(): jnp.dot(hidden, contract_weight, preferred_element_type=jnp.float32)  15.1 us
    reduce_sum x8, other arithmetic, advance(): denominator_next = denominator_now * rescale + jnp.sum(exponent, axis=-1)  11 us
  transfers between devices with their start and end apart: 6, of which 6 were waited for; matrix products, arithmetic and copies ran while one was open for 4% of the time, Pallas kernels for 0%

profile of v1, /device:TPU:0, one launch (start us, length us, event | category | flops | bytes accessed | tf_op | source)
XLA Modules:
  0.0 291.1 jit_solution(15406287768047057123)
XLA Ops:
  6.5 2.9 %collective-permute-start = (bf16[1,1024,256]{2,1,0:T(8,128)(2,1)}, bf16[1,1024,256]{2,1,0:T(8,128)(2,1)S(1)}, u32[]{:S(2)}, u32[]{:S(2)}) collective-permute-start(bf16[1,1024,256]{2,1,0:T(8,128)(2,1)} %param.20), channel_id=1, source_target_pairs={{0,8},{8,16},{16,24},{24,0},{1,9},{9,17},{17,25},{25,1},{2,10},{10... | collective-permute-start | bytes 1572872 | tf_op jit(solution)/shard_map/ppermute | solution.py:112
  9.5 13.1 %collective-permute-done = bf16[1,1024,256]{2,1,0:T(8,128)(2,1)S(1)} collective-permute-done((bf16[1,1024,256]{2,1,0:T(8,128)(2,1)}, bf16[1,1024,256]{2,1,0:T(8,128)(2,1)S(1)}, u32[]{:S(2)}, u32[]{:S(2)}) %collective-permute-start) | collective-permute-done | bytes 524320 | tf_op jit(solution)/shard_map/ppermute | solution.py:112
  22.6 0.8 collective-permute-start.1
  23.4 13.3 %collective-permute-done.1 = bf16[1,1024,256]{2,1,0:T(8,128)(2,1)S(1)} collective-permute-done((bf16[1,1024,256]{2,1,0:T(8,128)(2,1)S(1)}, bf16[1,1024,256]{2,1,0:T(8,128)(2,1)S(1)}, u32[]{:S(2)}, u32[]{:S(2)}) %collective-permute-start.1) | collective-permute-done | bytes 524320 | tf_op jit(solution)/shard_map/ppermute | solution.py:112
  36.6 1.3 fusion.43
  39.9 9.8 %collective-permute-done.2 = bf16[1,1024,256]{2,1,0:T(8,128)(2,1)S(1)} collective-permute-done((bf16[1,1024,256]{2,1,0:T(8,128)(2,1)S(1)}, bf16[1,1024,256]{2,1,0:T(8,128)(2,1)S(1)}, u32[]{:S(2)}, u32[]{:S(2)}) %collective-permute-start.2) | collective-permute-done | bytes 524320 | tf_op jit(solution)/shard_map/ppermute | solution.py:112
  49.7 0.8 copy-done.3
  50.6 1.1 constant_dynamic-update-slice_fusion.4
  51.7 1.1 constant_dynamic-update-slice_fusion.3
  53.0 0.8 constant_dynamic-slice_fusion
  54.4 4.7 %fusion.30 = bf16[16,16,8,128]{3,2,1,0:T(8,128)(2,1)S(1)} fusion(bf16[2048,2048]{1,0:T(8,128)(2,1)} %param.23, bf16[1,128,2048]{2,1,0:T(8,128)(2,1)S(1)} %copy-done.1, f32[2048]{0:T(1024)S(1)} %copy-done.6, f32[2048]{0:T(1024)S(1)} %copy-done.7, f32[128]{0:T(128)S(1)} %add_rsqrt_fusion.1, f32[128]{0:T(128)S(1)} %broadcast_multiply_fusion.1), kind=kOutput, calls=%fused_computation.39 | convolution fusion | flops 1075576832 | bytes 9454592 | tf_op jit(solution)/shard_map/dot_general | solution.py:121
  60.5 40.5 %all-gather.6.cloned.1.call-done = bf16[1,8192,256]{2,1,0:T(8,128)(2,1)} async-done(((bf16[1,1024,256]{2,1,0:T(8,128)(2,1)}), bf16[1,8192,256]{2,1,0:T(8,128)(2,1)}) %all-gather.6.cloned.1.call-update) | async-done | bytes 4194320 | tf_op jit(solution)/shard_map/all_gather | solution.py:51
  101.0 62.7 %while.14 = (s32[]{:T(128)}, f32[128,16,128]{2,0,1:T(8,128)S(1)}, f32[128,16]{0,1:T(8,128)S(1)}, f32[128,16]{0,1:T(8,128)S(1)}, s32[8]{0:T(128)S(1)}, /*index=5*...) while((s32[]{:T(128)}, f32[128,16,128]{2,0,1:T(8,128)S(1)}, ...), condition=%wide.region_10.11_spmd, body=%wide.region_7.10_spmd.sunk | while | flops 1091047424 | bytes 28442832 | solution.py:76
  102.2 2.2 bitcast_reduce_fusion.2
  104.4 1.4 fusion.68
  105.8 2.9 %fusion.69 = f32[128,16,128]{2,0,1:T(8,128)S(1)} fusion(f32[1024,128,16]{1,0,2:T(8,128)S(1)} %get-tuple-element.128, f32[128,16]{0,1:T(8,128)S(1)} %max.4, f32[128,16,128]{2,0,1:T(8,128)S(1)} %get-tuple-element.145, f32[128,16]{0,1:T(8,128)S(1)} %get-tuple-element.130, bf16[8192,256]{1,0:T(8,128)(2,1)} %get-tuple-element.161, s32[]{:T(128)S(6)} %select_n.67, ...), kind=kOutput, calls=%fused_computation.8.clone.1 | convolution fusion | flops 543686656 | bytes 10764296 | tf_op jit(solution)/shard_map/while/body/eval_jaxpr/thp,pd->thd/dot_general | solution.py:68
  110.0 2.2 bitcast_reduce_fusion.2
  112.3 1.4 fusion.68
  113.7 2.9 %fusion.69 = f32[128,16,128]{2,0,1:T(8,128)S(1)} fusion(f32[1024,128,16]{1,0,2:T(8,128)S(1)} %get-tuple-element.128, f32[128,16]{0,1:T(8,128)S(1)} %max.4, f32[128,16,128]{2,0,1:T(8,128)S(1)} %get-tuple-element.145, f32[128,16]{0,1:T(8,128)S(1)} %get-tuple-element.130, bf16[8192,256]{1,0:T(8,128)(2,1)} %get-tuple-element.161, s32[]{:T(128)S(6)} %select_n.67, ...), kind=kOutput, calls=%fused_computation.8.clone.1 | convolution fusion | flops 543686656 | bytes 10764296 | tf_op jit(solution)/shard_map/while/body/eval_jaxpr/thp,pd->thd/dot_general | solution.py:68
  117.9 2.2 bitcast_reduce_fusion.2
  120.1 1.4 fusion.68
  121.5 2.9 %fusion.69 = f32[128,16,128]{2,0,1:T(8,128)S(1)} fusion(f32[1024,128,16]{1,0,2:T(8,128)S(1)} %get-tuple-element.128, f32[128,16]{0,1:T(8,128)S(1)} %max.4, f32[128,16,128]{2,0,1:T(8,128)S(1)} %get-tuple-element.145, f32[128,16]{0,1:T(8,128)S(1)} %get-tuple-element.130, bf16[8192,256]{1,0:T(8,128)(2,1)} %get-tuple-element.161, s32[]{:T(128)S(6)} %select_n.67, ...), kind=kOutput, calls=%fused_computation.8.clone.1 | convolution fusion | flops 543686656 | bytes 10764296 | tf_op jit(solution)/shard_map/while/body/eval_jaxpr/thp,pd->thd/dot_general | solution.py:68
  125.7 2.2 bitcast_reduce_fusion.2
  128.0 1.4 fusion.68
  129.4 2.9 %fusion.69 = f32[128,16,128]{2,0,1:T(8,128)S(1)} fusion(f32[1024,128,16]{1,0,2:T(8,128)S(1)} %get-tuple-element.128, f32[128,16]{0,1:T(8,128)S(1)} %max.4, f32[128,16,128]{2,0,1:T(8,128)S(1)} %get-tuple-element.145, f32[128,16]{0,1:T(8,128)S(1)} %get-tuple-element.130, bf16[8192,256]{1,0:T(8,128)(2,1)} %get-tuple-element.161, s32[]{:T(128)S(6)} %select_n.67, ...), kind=kOutput, calls=%fused_computation.8.clone.1 | convolution fusion | flops 543686656 | bytes 10764296 | tf_op jit(solution)/shard_map/while/body/eval_jaxpr/thp,pd->thd/dot_general | solution.py:68
  133.6 2.2 bitcast_reduce_fusion.2
  135.8 1.4 fusion.68
  137.2 2.9 %fusion.69 = f32[128,16,128]{2,0,1:T(8,128)S(1)} fusion(f32[1024,128,16]{1,0,2:T(8,128)S(1)} %get-tuple-element.128, f32[128,16]{0,1:T(8,128)S(1)} %max.4, f32[128,16,128]{2,0,1:T(8,128)S(1)} %get-tuple-element.145, f32[128,16]{0,1:T(8,128)S(1)} %get-tuple-element.130, bf16[8192,256]{1,0:T(8,128)(2,1)} %get-tuple-element.161, s32[]{:T(128)S(6)} %select_n.67, ...), kind=kOutput, calls=%fused_computation.8.clone.1 | convolution fusion | flops 543686656 | bytes 10764296 | tf_op jit(solution)/shard_map/while/body/eval_jaxpr/thp,pd->thd/dot_general | solution.py:68
  141.4 2.2 bitcast_reduce_fusion.2
  143.6 1.4 fusion.68
  145.0 2.9 %fusion.69 = f32[128,16,128]{2,0,1:T(8,128)S(1)} fusion(f32[1024,128,16]{1,0,2:T(8,128)S(1)} %get-tuple-element.128, f32[128,16]{0,1:T(8,128)S(1)} %max.4, f32[128,16,128]{2,0,1:T(8,128)S(1)} %get-tuple-element.145, f32[128,16]{0,1:T(8,128)S(1)} %get-tuple-element.130, bf16[8192,256]{1,0:T(8,128)(2,1)} %get-tuple-element.161, s32[]{:T(128)S(6)} %select_n.67, ...), kind=kOutput, calls=%fused_computation.8.clone.1 | convolution fusion | flops 543686656 | bytes 10764296 | tf_op jit(solution)/shard_map/while/body/eval_jaxpr/thp,pd->thd/dot_general | solution.py:68
  149.3 2.2 bitcast_reduce_fusion.2
  151.5 1.4 fusion.68
  152.9 2.9 %fusion.69 = f32[128,16,128]{2,0,1:T(8,128)S(1)} fusion(f32[1024,128,16]{1,0,2:T(8,128)S(1)} %get-tuple-element.128, f32[128,16]{0,1:T(8,128)S(1)} %max.4, f32[128,16,128]{2,0,1:T(8,128)S(1)} %get-tuple-element.145, f32[128,16]{0,1:T(8,128)S(1)} %get-tuple-element.130, bf16[8192,256]{1,0:T(8,128)(2,1)} %get-tuple-element.161, s32[]{:T(128)S(6)} %select_n.67, ...), kind=kOutput, calls=%fused_computation.8.clone.1 | convolution fusion | flops 543686656 | bytes 10764296 | tf_op jit(solution)/shard_map/while/body/eval_jaxpr/thp,pd->thd/dot_general | solution.py:68
  157.1 2.2 bitcast_reduce_fusion.2
  159.3 1.4 fusion.68
  160.7 2.9 %fusion.69 = f32[128,16,128]{2,0,1:T(8,128)S(1)} fusion(f32[1024,128,16]{1,0,2:T(8,128)S(1)} %get-tuple-element.128, f32[128,16]{0,1:T(8,128)S(1)} %max.4, f32[128,16,128]{2,0,1:T(8,128)S(1)} %get-tuple-element.145, f32[128,16]{0,1:T(8,128)S(1)} %get-tuple-element.130, bf16[8192,256]{1,0:T(8,128)(2,1)} %get-tuple-element.161, s32[]{:T(128)S(6)} %select_n.67, ...), kind=kOutput, calls=%fused_computation.8.clone.1 | convolution fusion | flops 543686656 | bytes 10764296 | tf_op jit(solution)/shard_map/while/body/eval_jaxpr/thp,pd->thd/dot_general | solution.py:68
  163.7 1.3 copy.23
  165.0 1.3 divide_convert_fusion
  166.4 4.8 %fusion.51 = (f32[128]{0:T(128)S(1)}, f32[128,2048]{1,0:T(8,128)S(1)}) fusion(bf16[128,2048]{0,1:T(8,128)(2,1)S(1)} %bitcast.88, bf16[2048,2048]{1,0:T(8,128)(2,1)} %param.25, bf16[1,128,2048]{2,1,0:T(8,128)(2,1)S(1)} %copy-done.1), kind=kOutput, calls=%fused_computation.84 | convolution fusion | flops 1074528128 | bytes 10486272 | tf_op jit(solution)/shard_map/dot_general | solution.py:127
  171.5 1.0 add_convert_fusion
  172.8 45.8 %all-gather.4.cloned.1.call-done = bf16[1024,2048]{1,0:T(8,128)(2,1)} async-done(((bf16[128,2048]{1,0:T(8,128)(2,1)}), bf16[1024,2048]{1,0:T(8,128)(2,1)}) %all-gather.4.cloned.1.call-update) | async-done | bytes 4194320 | tf_op jit(solution)/shard_map/all_gather | solution.py:131
  218.6 15.1 %convolution_convert_fusion = bf16[1024,2048]{1,0:T(8,128)(2,1)} fusion(bf16[1024,2048]{1,0:T(8,128)(2,1)} %param.29, bf16[1024,2048]{1,0:T(8,128)(2,1)} %all-gather.4.cloned.1.call-done, bf16[2048,1024]{1,0:T(8,128)(2,1)} %param.28), kind=kOutput, calls=%fused_computation.25 | convolution fusion | flops 8601468928 | bytes 16777216 | tf_op jit(solution)/shard_map/dot_general | solution.py:138
  233.7 0.6 copy-done.8
  234.4 0.6 fusion.41
  235.0 1.2 fusion.42
  236.8 45.8 %reduce-scatter.2.cloned.1.call-done = bf16[128,2048]{1,0:T(8,128)(2,1)} async-done(((bf16[1024,2048]{1,0:T(8,128)(2,1)}), bf16[128,2048]{1,0:T(8,128)(2,1)}) %reduce-scatter.2.cloned.1.call-update) | async-done | bytes 524304 | tf_op jit(solution)/shard_map/reduce_scatter | solution.py:137
  282.6 2.0 fusion.39
  (78 shorter events, 8.1 us)
Async XLA Ops:
  6.5 52.7 %copy-start = (bf16[2048,256]{1,0:T(8,128)(2,1)S(1)}, bf16[2048,256]{1,0:T(8,128)(2,1)}, u32[]{:S(2)}) copy-start(bf16[2048,256]{1,0:T(8,128)(2,1)} %param.24) | copy-start | bytes 3145732
  6.5 46.4 %copy-start.2 = (bf16[1,1024,256]{2,1,0:T(8,128)(2,1)S(1)}, bf16[1,1024,256]{2,1,0:T(8,128)(2,1)}, u32[]{:S(2)}) copy-start(bf16[1,1024,256]{2,1,0:T(8,128)(2,1)} %param.20) | copy-start | bytes 1572868
  6.5 94.4 %all-gather.6.cloned.1.call-start = ((), (), s32[]{:S(2)}) async-start(), calls=%async_computation.3 | async-start | bytes 4718592 | tf_op jit(solution)/shard_map/all_gather | solution.py:51
  6.5 16.1 %collective-permute-start = (bf16[1,1024,256]{2,1,0:T(8,128)(2,1)}, bf16[1,1024,256]{2,1,0:T(8,128)(2,1)S(1)}, u32[]{:S(2)}, u32[]{:S(2)}) collective-permute-start(bf16[1,1024,256]{2,1,0:T(8,128)(2,1)} %param.20), channel_id=1, source_target_pairs={{0,8},{8,16},{16,24},{24,0},{1,9},{9,17},{17,25},{25,1},{2,10},{10... | collective-permute-start | bytes 1572872 | tf_op jit(solution)/shard_map/ppermute | solution.py:112
  22.6 14.0 %collective-permute-start.1 = (bf16[1,1024,256]{2,1,0:T(8,128)(2,1)S(1)}, bf16[1,1024,256]{2,1,0:T(8,128)(2,1)S(1)}, u32[]{:S(2)}, u32[]{:S(2)}) collective-permute-start(bf16[1,1024,256]{2,1,0:T(8,128)(2,1)S(1)} %collective-permute-done), channel_id=1, source_target_pairs={{0,8},{8,16},{16,24},{24,0},{1,9},{9,17},{17,25},{25,1},{2,10},{10... | collective-permute-start | bytes 1572872 | tf_op jit(solution)/shard_map/ppermute | solution.py:112
  36.6 13.1 %collective-permute-start.2 = (bf16[1,1024,256]{2,1,0:T(8,128)(2,1)S(1)}, bf16[1,1024,256]{2,1,0:T(8,128)(2,1)S(1)}, u32[]{:S(2)}, u32[]{:S(2)}) collective-permute-start(bf16[1,1024,256]{2,1,0:T(8,128)(2,1)S(1)} %collective-permute-done.1), channel_id=1, source_target_pairs={{0,8},{8,16},{16,24},{24,0},{1,9},{9,17},{17,25},{25,1},{2,10},{10... | collective-permute-start | bytes 1572872 | tf_op jit(solution)/shard_map/ppermute | solution.py:112
  49.7 0.8 copy-start.3
  50.5 3.3 %copy-start.1 = (bf16[1,128,2048]{2,1,0:T(8,128)(2,1)S(1)}, bf16[1,128,2048]{2,1,0:T(8,128)(2,1)}, u32[]{:S(2)}) copy-start(bf16[1,128,2048]{2,1,0:T(8,128)(2,1)} %param.16) | copy-start | bytes 1572868
  50.6 3.8 %copy-start.6 = (f32[2048]{0:T(1024)S(1)}, f32[2048]{0:T(1024)}, u32[]{:S(2)}) copy-start(f32[2048]{0:T(1024)} %param.22) | copy-start | bytes 24580
  50.6 3.8 %copy-start.7 = (f32[2048]{0:T(1024)S(1)}, f32[2048]{0:T(1024)}, u32[]{:S(2)}) copy-start(f32[2048]{0:T(1024)} %param.21) | copy-start | bytes 24580
  53.8 164.8 %all-gather.4.cloned.1.call-start = ((), (), s32[]{:S(2)}) async-start(), calls=%async_computation.1 | async-start | bytes 4718592 | tf_op jit(solution)/shard_map/all_gather | solution.py:131
  166.4 5.1 %copy-start.4 = (f32[2048]{0:T(1024)S(1)}, f32[2048]{0:T(1024)}, u32[]{:S(2)}) copy-start(f32[2048]{0:T(1024)} %param.27) | copy-start | bytes 24580
  166.4 5.1 %copy-start.5 = (f32[2048]{0:T(1024)S(1)}, f32[2048]{0:T(1024)}, u32[]{:S(2)}) copy-start(f32[2048]{0:T(1024)} %param.26) | copy-start | bytes 24580
  172.5 110.1 %reduce-scatter.2.cloned.1.call-start = ((), (), s32[]{:S(2)}) async-start(), calls=%async_computation.2 | async-start | bytes 4718592 | tf_op jit(solution)/shard_map/reduce_scatter | solution.py:137
  233.7 0.7 copy-start.8
  233.7 1.3 copy-start.9
Sparse Core Ops, SparseCore 0:
  53.9 46.9 all-gather.5
  172.7 45.8 all-gather.3
  233.9 48.7 reduce-scatter.1
